TPU v7x, 32 devices: a whole 2x2x4 slice. The times are simulated.
32 devices in a mesh: grp: 4 (over y, x), sub: 8 (over z, core).
Axes of the slice: x: 2, y: 2, z: 4, core: 2. Of those that a mesh axis runs over, the one named last changes fastest.
Arguments:
- right_side: float32 [24576, 160], P(('grp', 'sub')), may hold values from -6 to 6
- iterate_in: float32 [24576, 160], P(('grp', 'sub')), may hold values from -6 to 6
- diagonal: float32 [24576], P(('grp', 'sub')), may hold values from 1.5 to 4
- block_values: bfloat16 [32, 6, 3, 128, 128], P(('grp', 'sub')), may hold values from -0.125 to 0.125
- block_cols: int32 [32, 6, 3], P(('grp', 'sub')), may hold values from 0 to 5, as said below
- couple_left: bfloat16 [24576, 128], P(('grp', 'sub')), may hold values from -0.125 to 0.125
- couple_right: bfloat16 [24576, 128], P(('grp', 'sub')), may hold values from -0.125 to 0.125
- send_rows: int32 [32, 2, 128], P(('grp', 'sub')), may hold values from 0 to 767, as said below
- local_inverse: bfloat16 [32, 1024, 1024], P(('grp', 'sub')), may hold values from -0.3 to 2.3, as said below
- coarse_basis: bfloat16 [32, 1024, 32], P(('grp', 'sub')), may hold values from -0.1875 to 0.1875
- coarse_diag: float32 [32, 32, 32], P(('grp', 'sub')), may hold values from -54 to 59.5, as said below
- coarse_up: float32 [32, 32, 32], P(('grp', 'sub')), may hold values from -29.7 to 27
Outputs:
- iterate: float32 [24576, 160], P(('grp', 'sub'))
- residual: float32 [24576, 160], P(('grp', 'sub'))
Inputs may be any that keep to these rules, and one draw needn't show every extreme that they name: `block_cols`: the 3 column blocks of one row block are distinct. `send_rows`: the 256 rows listed for one subdomain are distinct. `local_inverse`: each block is symmetric positive definite. `coarse_diag`: each block is symmetric; with coarse_up the coarse operator is symmetric positive definite.
All inputs are finite; a program needn't handle non-finite values.
Results may differ from a plain program's by a relative error of at most 0.0032.
Values may be sent and summed in bfloat16 or wider, within the bound.
No kernel may reach another device: no remote copies, remote signals or barrier semaphores. Data moves between devices by JAX's collectives and lax.ppermute only.
A program may use at most 64 MiB of HBM per device.

v0:
```python
import jax
import jax.numpy as jnp
from jax import lax
from jax.sharding import PartitionSpec as P


def with_halo(cells, sides, width):
    for axis, dim in sides:
        count = lax.axis_size(axis)
        ends = count - 1
        head = lax.slice_in_dim(cells, 0, width, axis=dim)
        tail = lax.slice_in_dim(cells, cells.shape[dim] - width, cells.shape[dim], axis=dim)
        cells = jnp.concatenate(
            [
                lax.ppermute(tail, axis, [(i, (i + 1) % count) for i in range(ends)]),
                cells,
                lax.ppermute(head, axis, [((i + 1) % count, i) for i in range(ends)]),
            ],
            axis=dim,
        )
    return cells


def chol_solve(factor, values):
    halfway = lax.linalg.triangular_solve(factor, values, left_side=True, lower=True)
    return lax.linalg.triangular_solve(
        factor, halfway, left_side=True, lower=True, transpose_a=True
    )


def solve_chain(diagonal_blocks, upper, values):
    highest = lax.Precision.HIGHEST
    blocks_total = diagonal_blocks.shape[0]
    padded_total = 1
    while padded_total < blocks_total:
        padded_total = padded_total * 2
    extra = padded_total - blocks_total
    block_width = diagonal_blocks.shape[1]
    identity = jnp.eye(block_width, dtype=jnp.float32)
    diag_now = jnp.concatenate(
        [diagonal_blocks, jnp.broadcast_to(identity, (extra, block_width, block_width))], axis=0
    )
    upper_now = jnp.concatenate(
        [upper[:-1], jnp.zeros((extra + 1, block_width, block_width), jnp.float32)], axis=0
    )
    rhs_now = jnp.concatenate([values, jnp.zeros((extra,) + values.shape[1:], jnp.float32)], axis=0)
    levels = []
    while diag_now.shape[0] > 1:
        diag_even = diag_now[0::2]
        diag_odd = diag_now[1::2]
        upper_even = upper_now[0::2]
        upper_odd = upper_now[1::2]
        rhs_even = rhs_now[0::2]
        rhs_odd = rhs_now[1::2]
        factor = jnp.linalg.cholesky(diag_odd)
        stacked = jnp.concatenate([jnp.swapaxes(upper_even, 1, 2), upper_odd, rhs_odd], axis=2)
        through = chol_solve(factor, stacked)
        toward_left = through[:, :, :block_width]
        toward_right = through[:, :, block_width : 2 * block_width]
        odd_loads = through[:, :, 2 * block_width :]
        new_diag = diag_even - jnp.einsum(
            "mab,mbc->mac", upper_even, toward_left, precision=highest
        )
        new_upper = -jnp.einsum("mab,mbc->mac", upper_even, toward_right, precision=highest)
        new_rhs = rhs_even - jnp.einsum("mab,mbn->man", upper_even, odd_loads, precision=highest)
        from_diag = jnp.einsum("mba,mbc->mac", upper_odd, toward_right, precision=highest)
        from_rhs = jnp.einsum("mba,mbn->man", upper_odd, odd_loads, precision=highest)
        new_diag = new_diag - jnp.concatenate(
            [jnp.zeros_like(from_diag[:1]), from_diag[:-1]], axis=0
        )
        new_rhs = new_rhs - jnp.concatenate([jnp.zeros_like(from_rhs[:1]), from_rhs[:-1]], axis=0)
        levels.append((toward_left, toward_right, odd_loads))
        diag_now, upper_now, rhs_now = (new_diag, new_upper, new_rhs)
    solution = chol_solve(jnp.linalg.cholesky(diag_now[0]), rhs_now[0])[None]
    for toward_left, toward_right, odd_loads in reversed(levels):
        next_sol = jnp.concatenate([solution[1:], jnp.zeros_like(solution[:1])], axis=0)
        odd_part = (
            odd_loads
            - jnp.einsum("mab,mbn->man", toward_left, solution, precision=highest)
            - jnp.einsum("mab,mbn->man", toward_right, next_sol, precision=highest)
        )
        solution = jnp.stack([solution, odd_part], axis=1).reshape((-1,) + solution.shape[1:])
    return solution[:blocks_total]


def shards(
    right_side,
    iterate_in,
    diagonal,
    block_values,
    block_cols,
    couple_left,
    couple_right,
    send_rows,
    local_inverse,
    coarse_basis,
    coarse_diag,
    coarse_up,
):
    bf16 = jnp.bfloat16
    f32 = jnp.float32
    highest = lax.Precision.HIGHEST
    intersection = send_rows.shape[2]
    rows_own = right_side.shape[0]
    cases = right_side.shape[1]
    row_blocks = block_cols.shape[1]
    modes = coarse_basis.shape[2]
    column_blocks = block_cols[0]
    sent_left_rows = send_rows[0, 0]
    sent_right_rows = send_rows[0, 1]

    def neighbour_rows(source):
        boundary = jnp.stack([source[sent_left_rows], source[sent_right_rows]])
        padded = with_halo(boundary, ((("grp", "sub"), 0),), 1)
        return (padded[0], padded[3])

    def apply_operator(vector):
        rounded = vector.astype(bf16)
        from_left, from_right = neighbour_rows(rounded)
        blocks = rounded.reshape(row_blocks, -1, cases)
        picked = blocks[column_blocks]
        sparse = jnp.einsum(
            "itab,itbn->ian", block_values[0], picked, preferred_element_type=f32
        ).reshape(rows_own, cases)
        coupled = jnp.dot(couple_left, from_left, preferred_element_type=f32) + jnp.dot(
            couple_right, from_right, preferred_element_type=f32
        )
        return diagonal[:, None] * vector + (sparse + coupled)

    residual_start = right_side - apply_operator(iterate_in)
    rounded = residual_start.astype(bf16)
    from_left, from_right = neighbour_rows(rounded)
    extended = jnp.concatenate([from_left, rounded, from_right], axis=0)
    local_part = jnp.dot(local_inverse[0], extended, preferred_element_type=f32)
    coarse_in = jnp.dot(coarse_basis[0].T, extended, preferred_element_type=f32)
    blocks_diag = lax.all_gather(coarse_diag, "sub", axis=0, tiled=True)
    blocks_up = lax.all_gather(coarse_up, "sub", axis=0, tiled=True)
    group = lax.axis_index("grp")
    groups = lax.axis_size("grp")
    member = lax.axis_index("sub")
    members = lax.axis_size("sub")
    keep = (group < groups - 1).astype(f32)
    first_up = blocks_up[0]
    last_up = blocks_up[members - 1] * keep
    columns = lax.all_gather(coarse_in[None], "sub", axis=0, tiled=True)
    width = columns.shape[2]
    inner_count = members - 1
    empty_cols = jnp.zeros((inner_count, modes, modes), f32)
    left_cols = empty_cols.at[0].set(first_up.T)
    right_cols = empty_cols.at[inner_count - 1].set(last_up)
    stacked = jnp.concatenate([columns[1:], left_cols, right_cols], axis=2)
    solved = solve_chain(blocks_diag[1:], blocks_up[1:], stacked)
    sol_loads = solved[:, :, :width]
    sol_left = solved[:, :, width : width + modes]
    sol_right = solved[:, :, width + modes :]
    self_left = jnp.dot(first_up, sol_left[0], precision=highest)
    cross_term = jnp.dot(first_up, sol_right[0], precision=highest)
    rhs_first = jnp.dot(first_up, sol_loads[0], precision=highest)
    self_right = jnp.dot(last_up.T, sol_right[-1], precision=highest)
    rhs_last = jnp.dot(last_up.T, sol_loads[-1], precision=highest)
    sep_diag = lax.all_gather(blocks_diag[0][None], "grp", axis=0, tiled=True)
    sep_rhs = lax.all_gather(columns[0][None], "grp", axis=0, tiled=True)
    all_left = lax.all_gather(self_left[None], "grp", axis=0, tiled=True)
    all_right = lax.all_gather(self_right[None], "grp", axis=0, tiled=True)
    all_cross = lax.all_gather(cross_term[None], "grp", axis=0, tiled=True)
    all_first = lax.all_gather(rhs_first[None], "grp", axis=0, tiled=True)
    all_last = lax.all_gather(rhs_last[None], "grp", axis=0, tiled=True)
    prev_right = jnp.concatenate([jnp.zeros_like(all_right[:1]), all_right[:-1]], axis=0)
    prev_last = jnp.concatenate([jnp.zeros_like(all_last[:1]), all_last[:-1]], axis=0)
    reduced_diag = sep_diag - all_left - prev_right
    reduced_rhs = sep_rhs - all_first - prev_last
    sep_sol = solve_chain(reduced_diag, -all_cross, reduced_rhs)
    padded_sol = jnp.concatenate([sep_sol, jnp.zeros_like(sep_sol[:1])], axis=0)
    mine = lax.dynamic_index_in_dim(padded_sol, group, 0, keepdims=False)
    after = lax.dynamic_index_in_dim(padded_sol, group + 1, 0, keepdims=False)
    inner_sol = (
        sol_loads
        - jnp.einsum("ivw,wn->ivn", sol_left, mine, precision=highest)
        - jnp.einsum("ivw,wn->ivn", sol_right, after, precision=highest)
    )
    group_sol = jnp.concatenate([mine[None], inner_sol], axis=0)
    coarse_sol = lax.dynamic_index_in_dim(group_sol, member, 0, keepdims=False)
    correction = local_part + jnp.dot(
        coarse_basis[0], coarse_sol.astype(bf16), preferred_element_type=f32
    )
    tails = jnp.stack([correction[:intersection], correction[intersection + rows_own :]])
    returned = with_halo(tails.astype(jnp.bfloat16), ((("grp", "sub"), 0),), 1).astype(tails.dtype)
    owned = correction[intersection : intersection + rows_own]
    owned = owned.at[sent_right_rows].add(returned[3])
    owned = owned.at[sent_left_rows].add(returned[0])
    inner = lax.psum(jnp.sum(residual_start * owned, axis=0), ("grp", "sub"))
    image = apply_operator(owned)
    curvature = lax.psum(jnp.sum(owned * image, axis=0), ("grp", "sub"))
    step_size = inner / curvature
    return (iterate_in + step_size * owned, residual_start - step_size * image)


def solution(mesh):
    in_specs = (
        P(("grp", "sub"), None),
        P(("grp", "sub"), None),
        P(("grp", "sub")),
        P(("grp", "sub"), None, None, None, None),
        P(("grp", "sub"), None, None),
        P(("grp", "sub"), None),
        P(("grp", "sub"), None),
        P(("grp", "sub"), None, None),
        P(("grp", "sub"), None, None),
        P(("grp", "sub"), None, None),
        P(("grp", "sub"), None, None),
        P(("grp", "sub"), None, None),
    )
    out_specs = (P(("grp", "sub"), None), P(("grp", "sub"), None))
    return jax.shard_map(shards, mesh=mesh, in_specs=in_specs, out_specs=out_specs, check_vma=False)
```

profile of v0, /device:TPU:14, one launch (start us, length us, event | category | flops | bytes accessed | tf_op | source)
XLA Modules:
  0.0 289.2 jit_solution(11546375033526299166)
XLA Ops:
  7.7 2.4 collective-permute-start
  10.4 14.8 %all_gather.32 = f32[8,32,32]{2,1,0:T(8,128)S(1)} all-gather(f32[1,32,32]{2,1,0:T(8,128)S(1)} %copy-done.34), channel_id=1, replica_groups=mesh['grp'=4,'sub'=8] {'sub'}, dimensions={0}, use_global_device_ids=true | all-gather | bytes 36864 | tf_op jit(solution)/shard_map/all_gather | solution.py:137
  25.2 14.0 %all_gather.30 = f32[8,32,32]{2,1,0:T(8,128)S(1)} all-gather(f32[1,32,32]{2,1,0:T(8,128)S(1)} %copy-done.35), channel_id=1, replica_groups=mesh['grp'=4,'sub'=8] {'sub'}, dimensions={0}, use_global_device_ids=true | all-gather | bytes 36864 | tf_op jit(solution)/shard_map/all_gather | solution.py:136
  39.5 11.7 %custom-call.47 = f32[4,32,32]{2,1,0:T(8,128)S(1)} custom-call(f32[4,32,32]{2,1,0:T(8,128)S(1)} %copy.185), custom_call_target="Cholesky" | custom-call | tf_op jit(solution)/shard_map/jit(cholesky)/cholesky | solution.py:55
  61.8 4.0 %collective-permute-start.3 = (bf16[1,128,160]{1,2,0:T(8,128)(2,1)S(1)}, bf16[1,128,160]{1,2,0:T(8,128)(2,1)S(1)}, u32[]{:S(2)}, u32[]{:S(2)}) collective-permute-start(bf16[1,128,160]{1,2,0:T(8,128)(2,1)S(1)} %bitcast.412), channel_id=1, source_target_pairs={{1,0},{2,1},{3,2},{4,3},{5,4},{6,5},{7,6},{8,7},{9,8},{10,9},{11,1... | collective-permute-start | bytes 122888 | tf_op jit(solution)/shard_map/ppermute | solution.py:17
  68.7 11.2 %custom-call.48 = f32[4,1,32,32]{2,3,1,0:T(8,128)} custom-call(f32[4,1,32,32]{3,2,1,0:T(8,128)} %select_bitcast_fusion), custom_call_target="InvertDiagBlocksLowerTriangular" | custom-call | tf_op jit(solution)/shard_map/triangular_solve | solution.py:26
  79.9 9.1 %all_gather.31 = f32[4,32,32]{2,1,0:T(8,128)S(1)} all-gather(f32[1,32,32]{2,1,0:T(8,128)S(1)} %slice-done.1), channel_id=1, replica_groups=mesh['grp'=4,'sub'=8] {'grp'}, dimensions={0}, use_global_device_ids=true | all-gather | bytes 20480 | tf_op jit(solution)/shard_map/all_gather | solution.py:161
  90.5 12.7 %all-gather = f32[256,160]{1,0:T(8,128)S(1)} all-gather(f32[32,160]{1,0:T(8,128)S(1)} %convolution_bitcast_fusion.11), channel_id=2, replica_groups=mesh['grp'=4,'sub'=8] {'sub'}, dimensions={0}, use_global_device_ids=true | all-gather | bytes 184320 | tf_op jit(solution)/shard_map/all_gather | solution.py:145
  106.0 5.9 %custom-call.57 = f32[2,32,32]{2,1,0:T(8,128)S(1)} custom-call(f32[2,32,32]{2,1,0:T(8,128)S(1)} %fusion.117), custom_call_target="Cholesky" | custom-call | tf_op jit(solution)/shard_map/jit(cholesky)/cholesky | solution.py:55
  112.1 4.9 %custom-call.49 = f32[2,1,32,32]{2,3,1,0:T(8,128)S(1)} custom-call(f32[2,1,32,32]{3,2,1,0:T(8,128)S(1)} %fusion.119), custom_call_target="InvertDiagBlocksLowerTriangular" | custom-call | tf_op jit(solution)/shard_map/triangular_solve | solution.py:26
  119.1 2.9 %custom-call.58 = f32[1,32,32]{2,1,0:T(8,128)S(1)} custom-call(f32[1,32,32]{2,1,0:T(8,128)S(1)} %fusion.169), custom_call_target="Cholesky" | custom-call | tf_op jit(solution)/shard_map/jit(cholesky)/cholesky | solution.py:55
  123.2 2.4 custom-call.50
  126.9 2.9 %cholesky.184 = f32[32,32]{1,0:T(8,128)S(1)} custom-call(f32[32,32]{1,0:T(8,128)S(1)} %fusion.150), custom_call_target="Cholesky" | custom-call | tf_op jit(solution)/shard_map/jit(cholesky)/cholesky | solution.py:74
  131.1 2.4 custom-call.51
  136.5 7.0 %all-gather.6 = f32[128,160]{1,0:T(8,128)S(1)} all-gather(f32[32,160]{1,0:T(8,128)S(1)} %slice-done), channel_id=8, replica_groups=mesh['grp'=4,'sub'=8] {'grp'}, dimensions={0}, use_global_device_ids=true | all-gather | bytes 102400 | tf_op jit(solution)/shard_map/all_gather | solution.py:162
  143.4 8.9 %all-gather.4 = f32[128,160]{1,0:T(8,128)S(1)} all-gather(f32[32,160]{1,0:T(8,128)S(1)} %convolution_bitcast_fusion.7), channel_id=6, replica_groups=mesh['grp'=4,'sub'=8] {'grp'}, dimensions={0}, use_global_device_ids=true | all-gather | bytes 102400 | tf_op jit(solution)/shard_map/all_gather | solution.py:166
  152.4 7.1 %all-gather.5 = f32[128,160]{1,0:T(8,128)S(1)} all-gather(f32[32,160]{1,0:T(8,128)S(1)} %fusion.101), channel_id=7, replica_groups=mesh['grp'=4,'sub'=8] {'grp'}, dimensions={0}, use_global_device_ids=true | all-gather | bytes 102400 | tf_op jit(solution)/shard_map/all_gather | solution.py:167
  159.6 8.7 %all-gather.3 = f32[128,32]{1,0:T(8,128)S(1)} all-gather(f32[32,32]{1,0:T(8,128)S(1)} %copy.214), channel_id=5, replica_groups=mesh['grp'=4,'sub'=8] {'grp'}, dimensions={0}, use_global_device_ids=true | all-gather | bytes 20480 | tf_op jit(solution)/shard_map/all_gather | solution.py:165
  168.5 6.7 %all-gather.2 = f32[128,32]{1,0:T(8,128)S(1)} all-gather(f32[32,32]{1,0:T(8,128)S(1)} %fusion.145), channel_id=4, replica_groups=mesh['grp'=4,'sub'=8] {'grp'}, dimensions={0}, use_global_device_ids=true | all-gather | bytes 20480 | tf_op jit(solution)/shard_map/all_gather | solution.py:164
  175.4 8.9 %all-gather.1 = f32[128,32]{1,0:T(8,128)S(1)} all-gather(f32[32,32]{1,0:T(8,128)S(1)} %copy.208), channel_id=3, replica_groups=mesh['grp'=4,'sub'=8] {'grp'}, dimensions={0}, use_global_device_ids=true | all-gather | bytes 20480 | tf_op jit(solution)/shard_map/all_gather | solution.py:163
  184.6 5.9 %custom-call.59 = f32[2,32,32]{2,1,0:T(8,128)S(1)} custom-call(f32[2,32,32]{2,1,0:T(8,128)S(1)} %fusion.112), custom_call_target="Cholesky" | custom-call | tf_op jit(solution)/shard_map/jit(cholesky)/cholesky | solution.py:55
  190.7 4.9 %custom-call.52 = f32[2,1,32,32]{2,3,1,0:T(8,128)S(1)} custom-call(f32[2,1,32,32]{3,2,1,0:T(8,128)S(1)} %fusion.118), custom_call_target="InvertDiagBlocksLowerTriangular" | custom-call | tf_op jit(solution)/shard_map/triangular_solve | solution.py:26
  197.6 2.9 %custom-call.60 = f32[1,32,32]{2,1,0:T(8,128)S(1)} custom-call(f32[1,32,32]{2,1,0:T(8,128)S(1)} %fusion.158), custom_call_target="Cholesky" | custom-call | tf_op jit(solution)/shard_map/jit(cholesky)/cholesky | solution.py:55
  201.9 2.4 custom-call.53
  205.5 2.9 %cholesky.216 = f32[32,32]{1,0:T(8,128)S(1)} custom-call(f32[32,32]{1,0:T(8,128)S(1)} %fusion.149), custom_call_target="Cholesky" | custom-call | tf_op jit(solution)/shard_map/jit(cholesky)/cholesky | solution.py:74
  209.8 2.4 custom-call.54
  217.3 2.4 collective-permute-start.4
  220.1 4.3 %collective-permute-done.4 = bf16[1,128,160]{1,2,0:T(8,128)(2,1)S(1)} collective-permute-done((bf16[1,128,160]{1,2,0:T(8,128)(2,1)S(1)}, bf16[1,128,160]{1,2,0:T(8,128)(2,1)S(1)}, u32[]{:S(2)}, u32[]{:S(2)}) %collective-permute-start.4) | collective-permute-done | bytes 40992 | tf_op jit(solution)/shard_map/ppermute | solution.py:15
  233.4 2.4 collective-permute-start.6
  238.6 3.1 %collective-permute-done.6 = bf16[1,128,160]{2,1,0:T(8,128)(2,1)S(1)} collective-permute-done((bf16[1,128,160]{2,1,0:T(8,128)(2,1)S(1)}, bf16[1,128,160]{2,1,0:T(8,128)(2,1)S(1)}, u32[]{:S(2)}, u32[]{:S(2)}) %collective-permute-start.6) | collective-permute-done | bytes 40992 | tf_op jit(solution)/shard_map/ppermute | solution.py:15
  242.8 44.1 %all-reduce.16 = (f32[160]{0:T(256)S(1)}, f32[160]{0:T(256)S(1)}) all-reduce(f32[160]{0:T(256)S(1)} %get-tuple-element.30, f32[160]{0:T(256)S(1)} %get-tuple-element.29), channel_id=1, replica_groups=mesh['grp'=4,'sub'=8] {'grp','sub'}, use_global_device_ids=true, to_apply=%region_11.15 | all-reduce | flops 320 | bytes 2560 | tf_op jit(solution)/shard_map/psum | solution.py:191
  286.9 2.3 multiply_subtract_fusion
  (282 shorter events, 58.2 us)
Async XLA Ops:
  0.6 213.9 %copy-start = (bf16[1,1024,1024]{2,1,0:T(8,128)(2,1)S(1)}, bf16[1,1024,1024]{2,1,0:T(8,128)(2,1)}, u32[]{:S(2)}) copy-start(bf16[1,1024,1024]{2,1,0:T(8,128)(2,1)} %param.27) | copy-start | bytes 6291460
  0.6 9.5 %copy-start.43 = (s32[1,6,3]{1,0,2:T(1,128)S(1)}, s32[1,6,3]{1,0,2:T(1,128)}, u32[]{:S(2)}) copy-start(s32[1,6,3]{1,0,2:T(1,128)} %param.23) | copy-start | bytes 220
  0.7 9.7 %copy-start.34 = (f32[1,32,32]{2,1,0:T(8,128)S(1)}, f32[1,32,32]{2,1,0:T(8,128)}, u32[]{:S(2)}) copy-start(f32[1,32,32]{2,1,0:T(8,128)} %param.30) | copy-start | bytes 12292
  0.7 24.5 %copy-start.35 = (f32[1,32,32]{2,1,0:T(8,128)S(1)}, f32[1,32,32]{2,1,0:T(8,128)}, u32[]{:S(2)}) copy-start(f32[1,32,32]{2,1,0:T(8,128)} %param.29) | copy-start | bytes 12292
  2.8 7.3 %copy-start.38 = (s32[128]{0:T(128)}, s32[128]{0:T(128)S(1)}, u32[]{:S(2)}) copy-start(s32[128]{0:T(128)S(1)} %get-tuple-element.52) | copy-start | bytes 1540
  2.8 22.4 %copy-start.40 = (s32[128]{0:T(128)}, s32[128]{0:T(128)S(1)}, u32[]{:S(2)}) copy-start(s32[128]{0:T(128)S(1)} %get-tuple-element.51) | copy-start | bytes 1540
  2.8 22.4 %copy-start.36 = (s32[1024]{0:T(1024)}, s32[1024]{0:T(1024)S(1)}, u32[]{:S(2)}) copy-start(s32[1024]{0:T(1024)S(1)} %get-tuple-element.59) | copy-start | bytes 12292
  2.8 22.4 %copy-start.37 = (s32[1024]{0:T(1024)}, s32[1024]{0:T(1024)S(1)}, u32[]{:S(2)}) copy-start(s32[1024]{0:T(1024)S(1)} %get-tuple-element.58) | copy-start | bytes 12292
  4.3 52.1 %collective-permute-start.1 = (bf16[1,128,160]{2,1,0:T(8,128)(2,1)}, bf16[1,128,160]{2,1,0:T(8,128)(2,1)}, u32[]{:S(2)}, u32[]{:S(2)}) collective-permute-start(bf16[1,128,160]{2,1,0:T(8,128)(2,1)} %bitcast.13), channel_id=1, source_target_pairs={{1,0},{2,1},{3,2},{4,3},{5,4},{6,5},{7,6},{8,7},{9,8},{10,9},{11,1... | collective-permute-start | bytes 122888 | tf_op jit(solution)/shard_map/ppermute | solution.py:17
  7.7 49.8 %collective-permute-start = (bf16[1,128,160]{2,1,0:T(8,128)(2,1)}, bf16[1,128,160]{2,1,0:T(8,128)(2,1)}, u32[]{:S(2)}, u32[]{:S(2)}) collective-permute-start(bf16[1,128,160]{2,1,0:T(8,128)(2,1)} %bitcast.9), channel_id=1, source_target_pairs={{0,1},{1,2},{2,3},{3,4},{4,5},{5,6},{6,7},{7,8},{8,9},{9,10},{10,1... | collective-permute-start | bytes 122888 | tf_op jit(solution)/shard_map/ppermute | solution.py:15
  10.1 43.6 %copy-start.24 = (pred[32,32]{1,0:T(8,128)(4,1)}, pred[32,32]{1,0:T(8,128)(4,1)S(1)}, u32[]{:S(2)}) copy-start(pred[32,32]{1,0:T(8,128)(4,1)S(1)} %iota_compare_fusion.3) | copy-start | bytes 3076
  10.2 45.5 %copy-start.22 = (pred[32,32]{1,0:T(8,128)(4,1)}, pred[32,32]{1,0:T(8,128)(4,1)S(1)}, u32[]{:S(2)}) copy-start(pred[32,32]{1,0:T(8,128)(4,1)S(1)} %iota_compare_fusion.7) | copy-start | bytes 3076
  10.4 43.3 %copy-start.30 = (s32[1024]{0:T(1024)}, s32[1024]{0:T(1024)S(1)}, u32[]{:S(2)}) copy-start(s32[1024]{0:T(1024)S(1)} %pad_clamp_fusion.2) | copy-start | bytes 12292
  39.2 12.7 %copy-start.11 = (f32[8,32,32]{2,1,0:T(8,128)}, f32[8,32,32]{2,1,0:T(8,128)S(1)}, u32[]{:S(2)}) copy-start(f32[8,32,32]{2,1,0:T(8,128)S(1)} %all_gather.30) | copy-start | bytes 98308
  56.4 46.9 %copy-start.13 = (f32[1,32,32]{2,1,0:T(8,128)}, f32[1,32,32]{2,1,0:T(8,128)S(1)}, u32[]{:S(2)}) copy-start(f32[1,32,32]{2,1,0:T(8,128)S(1)} %get-tuple-element.38) | copy-start | bytes 12292
  59.5 20.4 %slice-start.1 = ((f32[8,32,32]{2,1,0:T(8,128)}), f32[1,32,32]{2,1,0:T(8,128)S(1)}, s32[]{:S(2)}) async-start(f32[8,32,32]{2,1,0:T(8,128)} %copy-done.11), calls=%async_computation.1 | async-start | bytes 32768 | tf_op jit(solution)/shard_map/slice | solution.py:161
  59.6 30.7 %copy-start.20 = (bf16[1,1024,32]{1,2,0:T(8,128)(2,1)S(1)}, bf16[1,1024,32]{1,2,0:T(8,128)(2,1)}, u32[]{:S(2)}) copy-start(bf16[1,1024,32]{1,2,0:T(8,128)(2,1)} %param.28) | copy-start | bytes 196612
  61.8 27.9 %collective-permute-start.3 = (bf16[1,128,160]{1,2,0:T(8,128)(2,1)S(1)}, bf16[1,128,160]{1,2,0:T(8,128)(2,1)S(1)}, u32[]{:S(2)}, u32[]{:S(2)}) collective-permute-start(bf16[1,128,160]{1,2,0:T(8,128)(2,1)S(1)} %bitcast.412), channel_id=1, source_target_pairs={{1,0},{2,1},{3,2},{4,3},{5,4},{6,5},{7,6},{8,7},{9,8},{10,9},{11,1... | collective-permute-start | bytes 122888 | tf_op jit(solution)/shard_map/ppermute | solution.py:17
  65.9 23.7 %collective-permute-start.2 = (bf16[1,128,160]{1,2,0:T(8,128)(2,1)S(1)}, bf16[1,128,160]{1,2,0:T(8,128)(2,1)S(1)}, u32[]{:S(2)}, u32[]{:S(2)}) collective-permute-start(bf16[1,128,160]{1,2,0:T(8,128)(2,1)S(1)} %bitcast.413), channel_id=1, source_target_pairs={{0,1},{1,2},{2,3},{3,4},{4,5},{5,6},{6,7},{7,8},{8,9},{9,10},{10,1... | collective-permute-start | bytes 122888 | tf_op jit(solution)/shard_map/ppermute | solution.py:15
  90.3 13.0 %copy-start.18 = (f32[4,1,32,32]{2,3,1,0:T(8,128)S(1)}, f32[4,1,32,32]{2,3,1,0:T(8,128)}, u32[]{:S(2)}) copy-start(f32[4,1,32,32]{2,3,1,0:T(8,128)} %custom-call.48) | copy-start | bytes 49156
  90.3 13.1 %copy-start.19 = (f32[4,32,32]{2,1,0:T(8,128)S(1)}, f32[4,32,32]{2,1,0:T(8,128)}, u32[]{:S(2)}) copy-start(f32[4,32,32]{2,1,0:T(8,128)} %copy.187) | copy-start | bytes 49156
  104.5 7.3 %copy-start.25 = (pred[32,32]{1,0:T(8,128)(4,1)S(1)}, pred[32,32]{1,0:T(8,128)(4,1)}, u32[]{:S(2)}) copy-start(pred[32,32]{1,0:T(8,128)(4,1)} %copy-done.24) | copy-start | bytes 3076
  104.5 7.5 %copy-start.23 = (pred[32,32]{1,0:T(8,128)(4,1)S(1)}, pred[32,32]{1,0:T(8,128)(4,1)}, u32[]{:S(2)}) copy-start(pred[32,32]{1,0:T(8,128)(4,1)} %copy-done.22) | copy-start | bytes 3076
  135.2 33.1 %copy-start.44 = (pred[4]{0:T(512)(128)(4,1)S(1)}, pred[4]{0:T(512)(128)(4,1)}, u32[]{:S(2)}) copy-start(pred[4]{0:T(512)(128)(4,1)} %constant.263.clone.1) | copy-start | bytes 16
  152.4 32.1 %copy-start.17 = (f32[4,32,32]{1,2,0:T(8,128)S(1)}, f32[4,32,32]{1,2,0:T(8,128)}, u32[]{:S(2)}) copy-start(f32[4,32,32]{1,2,0:T(8,128)} %copy.210) | copy-start | bytes 49156
  215.4 4.7 %collective-permute-start.5 = (bf16[1,128,160]{1,2,0:T(8,128)(2,1)S(1)}, bf16[1,128,160]{1,2,0:T(8,128)(2,1)S(1)}, u32[]{:S(2)}, u32[]{:S(2)}) collective-permute-start(bf16[1,128,160]{1,2,0:T(8,128)(2,1)S(1)} %get-tuple-element.34), channel_id=1, source_target_pairs={{1,0},{2,1},{3,2},{4,3},{5,4},{6,5},{7,6},{8,7},{9,8},{10,9},{11,1... | collective-permute-start | bytes 122888 | tf_op jit(solution)/shard_map/ppermute | solution.py:17
  217.3 7.1 %collective-permute-start.4 = (bf16[1,128,160]{1,2,0:T(8,128)(2,1)S(1)}, bf16[1,128,160]{1,2,0:T(8,128)(2,1)S(1)}, u32[]{:S(2)}, u32[]{:S(2)}) collective-permute-start(bf16[1,128,160]{1,2,0:T(8,128)(2,1)S(1)} %get-tuple-element.33), channel_id=1, source_target_pairs={{0,1},{1,2},{2,3},{3,4},{4,5},{5,6},{6,7},{7,8},{8,9},{9,10},{10,1... | collective-permute-start | bytes 122888 | tf_op jit(solution)/shard_map/ppermute | solution.py:15
  228.9 7.1 %copy-start.31 = (s32[1024]{0:T(1024)S(1)}, s32[1024]{0:T(1024)}, u32[]{:S(2)}) copy-start(s32[1024]{0:T(1024)} %copy-done.30) | copy-start | bytes 12292
  231.4 6.9 %collective-permute-start.7 = (bf16[1,128,160]{2,1,0:T(8,128)(2,1)}, bf16[1,128,160]{2,1,0:T(8,128)(2,1)S(1)}, u32[]{:S(2)}, u32[]{:S(2)}) collective-permute-start(bf16[1,128,160]{2,1,0:T(8,128)(2,1)} %bitcast.124), channel_id=1, source_target_pairs={{1,0},{2,1},{3,2},{4,3},{5,4},{6,5},{7,6},{8,7},{9,8},{10,9},{11,1... | collective-permute-start | bytes 122888 | tf_op jit(solution)/shard_map/ppermute | solution.py:17
  233.4 8.3 %collective-permute-start.6 = (bf16[1,128,160]{2,1,0:T(8,128)(2,1)S(1)}, bf16[1,128,160]{2,1,0:T(8,128)(2,1)S(1)}, u32[]{:S(2)}, u32[]{:S(2)}) collective-permute-start(bf16[1,128,160]{2,1,0:T(8,128)(2,1)S(1)} %bitcast.407), channel_id=1, source_target_pairs={{0,1},{1,2},{2,3},{3,4},{4,5},{5,6},{6,7},{7,8},{8,9},{9,10},{10,1... | collective-permute-start | bytes 122888 | tf_op jit(solution)/shard_map/ppermute | solution.py:15
  236.7 4.9 %copy-start.3 = (f32[768,160]{0,1:T(8,128)S(1)}, f32[768,160]{0,1:T(8,128)}, u32[]{:S(2)}) copy-start(f32[768,160]{0,1:T(8,128)} %get-tuple-element.54) | copy-start | bytes 1474564
  241.7 45.2 %copy-start.2 = (f32[768,160]{0,1:T(8,128)S(1)}, f32[768,160]{0,1:T(8,128)}, u32[]{:S(2)}) copy-start(f32[768,160]{0,1:T(8,128)} %param.20) | copy-start | bytes 1474564
  (23 other events, 56.1 us)
where the time goes:
time: 290 us; the launch traced here: 289 us
  blocking collectives  142 us (49%)
  other arithmetic  79.4 us (27%)
  matrix products  21.8 us (8%)
  starting transfers between devices  18.9 us (7%)
  local copies, waits for them, and re-layouts  17.4 us (6%)
  waiting for transfers between devices  7.38 us (3%)
    psum x1, blocking collectives, shards(): inner = lax.psum(jnp.sum(residual_start * owned, axis=0), ('grp', 'sub'))  44.1 us
    another operation x15, other arithmetic, chol_solve(): lax.linalg.triangular_solve(factor, halfway, left_side=True, lower=True,...  34 us
    another operation x15, other arithmetic, solve_chain(): factor = jnp.linalg.cholesky(diag_odd)  31.6 us
    all_gather x1, blocking collectives, shards(): blocks_up = lax.all_gather(coarse_up, 'sub', axis=0, tiled=True)  14.8 us
    all_gather x1, blocking collectives, shards(): blocks_diag = lax.all_gather(coarse_diag, 'sub', axis=0, tiled=True)  14 us
    all_gather x1, blocking collectives, shards(): columns = lax.all_gather(coarse_in[None], 'sub', axis=0, tiled=True)  12.7 us
    ppermute x4, starting transfers between devices, with_halo(): lax.ppermute(head, axis, [((i + 1) % count, i) for i in range(ends)])  9.75 us
    ppermute x4, starting transfers between devices, with_halo(): lax.ppermute(tail, axis, [(i, (i + 1) % count) for i in range(ends)])  9.13 us
  transfers between devices with their start and end apart: 8, of which 2 were waited for; matrix products, arithmetic and copies ran while one was open for 12% of the time, Pallas kernels for 0%

commit v1 on v0

--- a/solution.py
+++ b/solution.py
@@ -188,7 +188,7 @@
     owned = correction[intersection : intersection + rows_own]
     owned = owned.at[sent_right_rows].add(returned[3])
     owned = owned.at[sent_left_rows].add(returned[0])
-    inner = lax.psum(jnp.sum(residual_start * owned, axis=0), ("grp", "sub"))
+    inner = lax.psum(lax.psum(jnp.sum(residual_start * owned, axis=0), "grp"), "sub")
     image = apply_operator(owned)
     curvature = lax.psum(jnp.sum(owned * image, axis=0), ("grp", "sub"))
     step_size = inner / curvature

time: 290 us -> 313 us (1.079)
  blocking collectives: 142 us -> 164 us
    psum x1 -> x3, blocking collectives: 44.1 us -> 65.7 us  [the longest x1 42.6 us: shards(): curvature = lax.psum(jnp.sum(owned * image, axis=0), ('grp', 'sub'))]
  transfers between devices with their start and end apart: 8 -> 8, of which waited for: 2 -> 2; matrix products, arithmetic and copies ran while one was open for 12% -> 11% of each run, Pallas kernels for 0% -> 0%
where the time goes in v1:
time: 313 us; the launch traced here: 311 us
  blocking collectives  164 us (52%)
  other arithmetic  79.4 us (25%)
  matrix products  21.8 us (7%)
  starting transfers between devices  18.9 us (6%)
  local copies, waits for them, and re-layouts  17.5 us (6%)
  waiting for transfers between devices  7.4 us (2%)
    psum x1, blocking collectives, shards(): curvature = lax.psum(jnp.sum(owned * image, axis=0), ('grp', 'sub'))  42.6 us
    another operation x15, other arithmetic, chol_solve(): lax.linalg.triangular_solve(factor, halfway, left_side=True, lower=True,...  34 us
    another operation x15, other arithmetic, solve_chain(): factor = jnp.linalg.cholesky(diag_odd)  31.6 us
    all_gather x1, blocking collectives, shards(): blocks_up = lax.all_gather(coarse_up, 'sub', axis=0, tiled=True)  14.8 us
    psum x1, blocking collectives, shards(): lax.psum(lax.psum(jnp.sum(residual_start * owned, axis=0), 'grp'), 'sub')  14.7 us
    all_gather x1, blocking collectives, shards(): blocks_diag = lax.all_gather(coarse_diag, 'sub', axis=0, tiled=True)  14 us
    all_gather x1, blocking collectives, shards(): columns = lax.all_gather(coarse_in[None], 'sub', axis=0, tiled=True)  12.7 us
    ppermute x4, starting transfers between devices, with_halo(): lax.ppermute(head, axis, [((i + 1) % count, i) for i in range(ends)])  9.75 us
  transfers between devices with their start and end apart: 8, of which 2 were waited for; matrix products, arithmetic and copies ran while one was open for 11% of the time, Pallas kernels for 0%

profile of v1, /device:TPU:14, one launch (start us, length us, event | category | flops | bytes accessed | tf_op | source)
XLA Modules:
  0.0 310.9 jit_solution(14239580568657559619)
XLA Ops:
  10.4 14.8 %all_gather.32 = f32[8,32,32]{2,1,0:T(8,128)S(1)} all-gather(f32[1,32,32]{2,1,0:T(8,128)S(1)} %copy-done.34), channel_id=1, replica_groups=mesh['grp'=4,'sub'=8] {'sub'}, dimensions={0}, use_global_device_ids=true | all-gather | bytes 36864 | tf_op jit(solution)/shard_map/all_gather | solution.py:137
  25.2 14.0 %all_gather.30 = f32[8,32,32]{2,1,0:T(8,128)S(1)} all-gather(f32[1,32,32]{2,1,0:T(8,128)S(1)} %copy-done.35), channel_id=1, replica_groups=mesh['grp'=4,'sub'=8] {'sub'}, dimensions={0}, use_global_device_ids=true | all-gather | bytes 36864 | tf_op jit(solution)/shard_map/all_gather | solution.py:136
  39.5 11.7 %custom-call.47 = f32[4,32,32]{2,1,0:T(8,128)S(1)} custom-call(f32[4,32,32]{2,1,0:T(8,128)S(1)} %copy.185), custom_call_target="Cholesky" | custom-call | tf_op jit(solution)/shard_map/jit(cholesky)/cholesky | solution.py:55
  61.9 4.0 %collective-permute-start.3 = (bf16[1,128,160]{1,2,0:T(8,128)(2,1)S(1)}, bf16[1,128,160]{1,2,0:T(8,128)(2,1)S(1)}, u32[]{:S(2)}, u32[]{:S(2)}) collective-permute-start(bf16[1,128,160]{1,2,0:T(8,128)(2,1)S(1)} %bitcast.412), channel_id=1, source_target_pairs={{1,0},{2,1},{3,2},{4,3},{5,4},{6,5},{7,6},{8,7},{9,8},{10,9},{11,1... | collective-permute-start | bytes 122888 | tf_op jit(solution)/shard_map/ppermute | solution.py:17
  68.7 11.2 %custom-call.48 = f32[4,1,32,32]{2,3,1,0:T(8,128)} custom-call(f32[4,1,32,32]{3,2,1,0:T(8,128)} %select_bitcast_fusion), custom_call_target="InvertDiagBlocksLowerTriangular" | custom-call | tf_op jit(solution)/shard_map/triangular_solve | solution.py:26
  79.9 9.1 %all_gather.31 = f32[4,32,32]{2,1,0:T(8,128)S(1)} all-gather(f32[1,32,32]{2,1,0:T(8,128)S(1)} %slice-done.1), channel_id=1, replica_groups=mesh['grp'=4,'sub'=8] {'grp'}, dimensions={0}, use_global_device_ids=true | all-gather | bytes 20480 | tf_op jit(solution)/shard_map/all_gather | solution.py:161
  90.6 12.7 %all-gather = f32[256,160]{1,0:T(8,128)S(1)} all-gather(f32[32,160]{1,0:T(8,128)S(1)} %convolution_bitcast_fusion.11), channel_id=2, replica_groups=mesh['grp'=4,'sub'=8] {'sub'}, dimensions={0}, use_global_device_ids=true | all-gather | bytes 184320 | tf_op jit(solution)/shard_map/all_gather | solution.py:145
  106.1 5.9 %custom-call.57 = f32[2,32,32]{2,1,0:T(8,128)S(1)} custom-call(f32[2,32,32]{2,1,0:T(8,128)S(1)} %fusion.117), custom_call_target="Cholesky" | custom-call | tf_op jit(solution)/shard_map/jit(cholesky)/cholesky | solution.py:55
  112.2 4.9 %custom-call.49 = f32[2,1,32,32]{2,3,1,0:T(8,128)S(1)} custom-call(f32[2,1,32,32]{3,2,1,0:T(8,128)S(1)} %fusion.119), custom_call_target="InvertDiagBlocksLowerTriangular" | custom-call | tf_op jit(solution)/shard_map/triangular_solve | solution.py:26
  119.2 2.9 custom-call.58
  123.3 2.4 custom-call.50
  127.0 2.9 cholesky.184
  131.1 2.4 custom-call.51
  136.5 7.0 %all-gather.6 = f32[128,160]{1,0:T(8,128)S(1)} all-gather(f32[32,160]{1,0:T(8,128)S(1)} %slice-done), channel_id=8, replica_groups=mesh['grp'=4,'sub'=8] {'grp'}, dimensions={0}, use_global_device_ids=true | all-gather | bytes 102400 | tf_op jit(solution)/shard_map/all_gather | solution.py:162
  143.5 8.9 %all-gather.4 = f32[128,160]{1,0:T(8,128)S(1)} all-gather(f32[32,160]{1,0:T(8,128)S(1)} %convolution_bitcast_fusion.7), channel_id=6, replica_groups=mesh['grp'=4,'sub'=8] {'grp'}, dimensions={0}, use_global_device_ids=true | all-gather | bytes 102400 | tf_op jit(solution)/shard_map/all_gather | solution.py:166
  152.5 7.1 %all-gather.5 = f32[128,160]{1,0:T(8,128)S(1)} all-gather(f32[32,160]{1,0:T(8,128)S(1)} %fusion.101), channel_id=7, replica_groups=mesh['grp'=4,'sub'=8] {'grp'}, dimensions={0}, use_global_device_ids=true | all-gather | bytes 102400 | tf_op jit(solution)/shard_map/all_gather | solution.py:167
  159.7 8.7 %all-gather.3 = f32[128,32]{1,0:T(8,128)S(1)} all-gather(f32[32,32]{1,0:T(8,128)S(1)} %copy.214), channel_id=5, replica_groups=mesh['grp'=4,'sub'=8] {'grp'}, dimensions={0}, use_global_device_ids=true | all-gather | bytes 20480 | tf_op jit(solution)/shard_map/all_gather | solution.py:165
  168.6 6.7 %all-gather.2 = f32[128,32]{1,0:T(8,128)S(1)} all-gather(f32[32,32]{1,0:T(8,128)S(1)} %fusion.145), channel_id=4, replica_groups=mesh['grp'=4,'sub'=8] {'grp'}, dimensions={0}, use_global_device_ids=true | all-gather | bytes 20480 | tf_op jit(solution)/shard_map/all_gather | solution.py:164
  175.5 8.9 %all-gather.1 = f32[128,32]{1,0:T(8,128)S(1)} all-gather(f32[32,32]{1,0:T(8,128)S(1)} %copy.208), channel_id=3, replica_groups=mesh['grp'=4,'sub'=8] {'grp'}, dimensions={0}, use_global_device_ids=true | all-gather | bytes 20480 | tf_op jit(solution)/shard_map/all_gather | solution.py:163
  184.7 5.9 %custom-call.59 = f32[2,32,32]{2,1,0:T(8,128)S(1)} custom-call(f32[2,32,32]{2,1,0:T(8,128)S(1)} %fusion.112), custom_call_target="Cholesky" | custom-call | tf_op jit(solution)/shard_map/jit(cholesky)/cholesky | solution.py:55
  190.8 4.9 %custom-call.52 = f32[2,1,32,32]{2,3,1,0:T(8,128)S(1)} custom-call(f32[2,1,32,32]{3,2,1,0:T(8,128)S(1)} %fusion.118), custom_call_target="InvertDiagBlocksLowerTriangular" | custom-call | tf_op jit(solution)/shard_map/triangular_solve | solution.py:26
  197.7 2.9 custom-call.60
  202.0 2.4 custom-call.53
  205.6 2.9 cholesky.216
  209.9 2.4 custom-call.54
  217.4 2.4 collective-permute-start.4
  220.1 4.3 %collective-permute-done.4 = bf16[1,128,160]{1,2,0:T(8,128)(2,1)S(1)} collective-permute-done((bf16[1,128,160]{1,2,0:T(8,128)(2,1)S(1)}, bf16[1,128,160]{1,2,0:T(8,128)(2,1)S(1)}, u32[]{:S(2)}, u32[]{:S(2)}) %collective-permute-start.4) | collective-permute-done | bytes 40992 | tf_op jit(solution)/shard_map/ppermute | solution.py:15
  233.5 2.4 collective-permute-start.6
  238.7 3.1 collective-permute-done.6
  242.9 8.4 %psum.21 = f32[160]{0:T(256)S(1)} all-reduce(f32[160]{0:T(256)S(1)} %get-tuple-element.30), channel_id=1, replica_groups=mesh['grp'=4,'sub'=8] {'grp'}, use_global_device_ids=true, to_apply=%region_11.15 | all-reduce | flops 160 | bytes 1280 | tf_op jit(solution)/shard_map/psum | solution.py:191
  251.3 14.7 %psum.22 = f32[160]{0:T(256)S(1)} all-reduce(f32[160]{0:T(256)S(1)} %psum.21), channel_id=1, replica_groups=mesh['grp'=4,'sub'=8] {'sub'}, use_global_device_ids=true, to_apply=%region_12.16 | all-reduce | flops 160 | bytes 1280 | tf_op jit(solution)/shard_map/psum | solution.py:191
  266.0 42.6 %psum.23 = f32[160]{0:T(256)S(1)} all-reduce(f32[160]{0:T(256)S(1)} %get-tuple-element.29), channel_id=1, replica_groups=mesh['grp'=4,'sub'=8] {'grp','sub'}, use_global_device_ids=true, to_apply=%region_14.18 | all-reduce | flops 160 | bytes 1280 | tf_op jit(solution)/shard_map/psum | solution.py:193
  (284 shorter events, 62.9 us)
Async XLA Ops:
  0.6 213.9 %copy-start = (bf16[1,1024,1024]{2,1,0:T(8,128)(2,1)S(1)}, bf16[1,1024,1024]{2,1,0:T(8,128)(2,1)}, u32[]{:S(2)}) copy-start(bf16[1,1024,1024]{2,1,0:T(8,128)(2,1)} %param.27) | copy-start | bytes 6291460
  0.6 9.5 %copy-start.43 = (s32[1,6,3]{1,0,2:T(1,128)S(1)}, s32[1,6,3]{1,0,2:T(1,128)}, u32[]{:S(2)}) copy-start(s32[1,6,3]{1,0,2:T(1,128)} %param.23) | copy-start | bytes 220
  0.7 9.7 %copy-start.34 = (f32[1,32,32]{2,1,0:T(8,128)S(1)}, f32[1,32,32]{2,1,0:T(8,128)}, u32[]{:S(2)}) copy-start(f32[1,32,32]{2,1,0:T(8,128)} %param.30) | copy-start | bytes 12292
  0.7 24.5 %copy-start.35 = (f32[1,32,32]{2,1,0:T(8,128)S(1)}, f32[1,32,32]{2,1,0:T(8,128)}, u32[]{:S(2)}) copy-start(f32[1,32,32]{2,1,0:T(8,128)} %param.29) | copy-start | bytes 12292
  2.8 7.3 %copy-start.38 = (s32[128]{0:T(128)}, s32[128]{0:T(128)S(1)}, u32[]{:S(2)}) copy-start(s32[128]{0:T(128)S(1)} %get-tuple-element.50) | copy-start | bytes 1540
  2.8 22.4 %copy-start.40 = (s32[128]{0:T(128)}, s32[128]{0:T(128)S(1)}, u32[]{:S(2)}) copy-start(s32[128]{0:T(128)S(1)} %get-tuple-element.49) | copy-start | bytes 1540
  2.8 22.4 %copy-start.36 = (s32[1024]{0:T(1024)}, s32[1024]{0:T(1024)S(1)}, u32[]{:S(2)}) copy-start(s32[1024]{0:T(1024)S(1)} %get-tuple-element.57) | copy-start | bytes 12292
  2.8 22.4 %copy-start.37 = (s32[1024]{0:T(1024)}, s32[1024]{0:T(1024)S(1)}, u32[]{:S(2)}) copy-start(s32[1024]{0:T(1024)S(1)} %get-tuple-element.56) | copy-start | bytes 12292
  4.3 52.1 %collective-permute-start.1 = (bf16[1,128,160]{2,1,0:T(8,128)(2,1)}, bf16[1,128,160]{2,1,0:T(8,128)(2,1)}, u32[]{:S(2)}, u32[]{:S(2)}) collective-permute-start(bf16[1,128,160]{2,1,0:T(8,128)(2,1)} %bitcast.13), channel_id=1, source_target_pairs={{1,0},{2,1},{3,2},{4,3},{5,4},{6,5},{7,6},{8,7},{9,8},{10,9},{11,1... | collective-permute-start | bytes 122888 | tf_op jit(solution)/shard_map/ppermute | solution.py:17
  7.7 49.9 %collective-permute-start = (bf16[1,128,160]{2,1,0:T(8,128)(2,1)}, bf16[1,128,160]{2,1,0:T(8,128)(2,1)}, u32[]{:S(2)}, u32[]{:S(2)}) collective-permute-start(bf16[1,128,160]{2,1,0:T(8,128)(2,1)} %bitcast.9), channel_id=1, source_target_pairs={{0,1},{1,2},{2,3},{3,4},{4,5},{5,6},{6,7},{7,8},{8,9},{9,10},{10,1... | collective-permute-start | bytes 122888 | tf_op jit(solution)/shard_map/ppermute | solution.py:15
  10.1 43.6 %copy-start.24 = (pred[32,32]{1,0:T(8,128)(4,1)}, pred[32,32]{1,0:T(8,128)(4,1)S(1)}, u32[]{:S(2)}) copy-start(pred[32,32]{1,0:T(8,128)(4,1)S(1)} %iota_compare_fusion.3) | copy-start | bytes 3076
  10.2 45.5 %copy-start.22 = (pred[32,32]{1,0:T(8,128)(4,1)}, pred[32,32]{1,0:T(8,128)(4,1)S(1)}, u32[]{:S(2)}) copy-start(pred[32,32]{1,0:T(8,128)(4,1)S(1)} %iota_compare_fusion.7) | copy-start | bytes 3076
  10.4 43.3 %copy-start.30 = (s32[1024]{0:T(1024)}, s32[1024]{0:T(1024)S(1)}, u32[]{:S(2)}) copy-start(s32[1024]{0:T(1024)S(1)} %pad_clamp_fusion.2) | copy-start | bytes 12292
  39.2 12.8 %copy-start.11 = (f32[8,32,32]{2,1,0:T(8,128)}, f32[8,32,32]{2,1,0:T(8,128)S(1)}, u32[]{:S(2)}) copy-start(f32[8,32,32]{2,1,0:T(8,128)S(1)} %all_gather.30) | copy-start | bytes 98308
  56.4 46.9 %copy-start.13 = (f32[1,32,32]{2,1,0:T(8,128)}, f32[1,32,32]{2,1,0:T(8,128)S(1)}, u32[]{:S(2)}) copy-start(f32[1,32,32]{2,1,0:T(8,128)S(1)} %get-tuple-element.36) | copy-start | bytes 12292
  59.5 20.4 %slice-start.1 = ((f32[8,32,32]{2,1,0:T(8,128)}), f32[1,32,32]{2,1,0:T(8,128)S(1)}, s32[]{:S(2)}) async-start(f32[8,32,32]{2,1,0:T(8,128)} %copy-done.11), calls=%async_computation.1 | async-start | bytes 32768 | tf_op jit(solution)/shard_map/slice | solution.py:161
  59.7 30.7 %copy-start.20 = (bf16[1,1024,32]{1,2,0:T(8,128)(2,1)S(1)}, bf16[1,1024,32]{1,2,0:T(8,128)(2,1)}, u32[]{:S(2)}) copy-start(bf16[1,1024,32]{1,2,0:T(8,128)(2,1)} %param.28) | copy-start | bytes 196612
  61.9 27.9 %collective-permute-start.3 = (bf16[1,128,160]{1,2,0:T(8,128)(2,1)S(1)}, bf16[1,128,160]{1,2,0:T(8,128)(2,1)S(1)}, u32[]{:S(2)}, u32[]{:S(2)}) collective-permute-start(bf16[1,128,160]{1,2,0:T(8,128)(2,1)S(1)} %bitcast.412), channel_id=1, source_target_pairs={{1,0},{2,1},{3,2},{4,3},{5,4},{6,5},{7,6},{8,7},{9,8},{10,9},{11,1... | collective-permute-start | bytes 122888 | tf_op jit(solution)/shard_map/ppermute | solution.py:17
  66.0 23.8 %collective-permute-start.2 = (bf16[1,128,160]{1,2,0:T(8,128)(2,1)S(1)}, bf16[1,128,160]{1,2,0:T(8,128)(2,1)S(1)}, u32[]{:S(2)}, u32[]{:S(2)}) collective-permute-start(bf16[1,128,160]{1,2,0:T(8,128)(2,1)S(1)} %bitcast.413), channel_id=1, source_target_pairs={{0,1},{1,2},{2,3},{3,4},{4,5},{5,6},{6,7},{7,8},{8,9},{9,10},{10,1... | collective-permute-start | bytes 122888 | tf_op jit(solution)/shard_map/ppermute | solution.py:15
  90.4 13.0 %copy-start.18 = (f32[4,1,32,32]{2,3,1,0:T(8,128)S(1)}, f32[4,1,32,32]{2,3,1,0:T(8,128)}, u32[]{:S(2)}) copy-start(f32[4,1,32,32]{2,3,1,0:T(8,128)} %custom-call.48) | copy-start | bytes 49156
  90.4 13.1 %copy-start.19 = (f32[4,32,32]{2,1,0:T(8,128)S(1)}, f32[4,32,32]{2,1,0:T(8,128)}, u32[]{:S(2)}) copy-start(f32[4,32,32]{2,1,0:T(8,128)} %copy.187) | copy-start | bytes 49156
  104.6 7.3 %copy-start.25 = (pred[32,32]{1,0:T(8,128)(4,1)S(1)}, pred[32,32]{1,0:T(8,128)(4,1)}, u32[]{:S(2)}) copy-start(pred[32,32]{1,0:T(8,128)(4,1)} %copy-done.24) | copy-start | bytes 3076
  104.6 7.5 %copy-start.23 = (pred[32,32]{1,0:T(8,128)(4,1)S(1)}, pred[32,32]{1,0:T(8,128)(4,1)}, u32[]{:S(2)}) copy-start(pred[32,32]{1,0:T(8,128)(4,1)} %copy-done.22) | copy-start | bytes 3076
  135.3 33.1 %copy-start.44 = (pred[4]{0:T(512)(128)(4,1)S(1)}, pred[4]{0:T(512)(128)(4,1)}, u32[]{:S(2)}) copy-start(pred[4]{0:T(512)(128)(4,1)} %constant.263.clone.1) | copy-start | bytes 16
  152.5 32.1 %copy-start.17 = (f32[4,32,32]{1,2,0:T(8,128)S(1)}, f32[4,32,32]{1,2,0:T(8,128)}, u32[]{:S(2)}) copy-start(f32[4,32,32]{1,2,0:T(8,128)} %copy.210) | copy-start | bytes 49156
  215.5 4.7 %collective-permute-start.5 = (bf16[1,128,160]{1,2,0:T(8,128)(2,1)S(1)}, bf16[1,128,160]{1,2,0:T(8,128)(2,1)S(1)}, u32[]{:S(2)}, u32[]{:S(2)}) collective-permute-start(bf16[1,128,160]{1,2,0:T(8,128)(2,1)S(1)} %get-tuple-element.32), channel_id=1, source_target_pairs={{1,0},{2,1},{3,2},{4,3},{5,4},{6,5},{7,6},{8,7},{9,8},{10,9},{11,1... | collective-permute-start | bytes 122888 | tf_op jit(solution)/shard_map/ppermute | solution.py:17
  217.4 7.1 %collective-permute-start.4 = (bf16[1,128,160]{1,2,0:T(8,128)(2,1)S(1)}, bf16[1,128,160]{1,2,0:T(8,128)(2,1)S(1)}, u32[]{:S(2)}, u32[]{:S(2)}) collective-permute-start(bf16[1,128,160]{1,2,0:T(8,128)(2,1)S(1)} %get-tuple-element.31), channel_id=1, source_target_pairs={{0,1},{1,2},{2,3},{3,4},{4,5},{5,6},{6,7},{7,8},{8,9},{9,10},{10,1... | collective-permute-start | bytes 122888 | tf_op jit(solution)/shard_map/ppermute | solution.py:15
  229.0 7.1 %copy-start.31 = (s32[1024]{0:T(1024)S(1)}, s32[1024]{0:T(1024)}, u32[]{:S(2)}) copy-start(s32[1024]{0:T(1024)} %copy-done.30) | copy-start | bytes 12292
  231.5 6.9 %collective-permute-start.7 = (bf16[1,128,160]{2,1,0:T(8,128)(2,1)}, bf16[1,128,160]{2,1,0:T(8,128)(2,1)S(1)}, u32[]{:S(2)}, u32[]{:S(2)}) collective-permute-start(bf16[1,128,160]{2,1,0:T(8,128)(2,1)} %bitcast.124), channel_id=1, source_target_pairs={{1,0},{2,1},{3,2},{4,3},{5,4},{6,5},{7,6},{8,7},{9,8},{10,9},{11,1... | collective-permute-start | bytes 122888 | tf_op jit(solution)/shard_map/ppermute | solution.py:17
  233.5 8.3 %collective-permute-start.6 = (bf16[1,128,160]{2,1,0:T(8,128)(2,1)S(1)}, bf16[1,128,160]{2,1,0:T(8,128)(2,1)S(1)}, u32[]{:S(2)}, u32[]{:S(2)}) collective-permute-start(bf16[1,128,160]{2,1,0:T(8,128)(2,1)S(1)} %bitcast.407), channel_id=1, source_target_pairs={{0,1},{1,2},{2,3},{3,4},{4,5},{5,6},{6,7},{7,8},{8,9},{9,10},{10,1... | collective-permute-start | bytes 122888 | tf_op jit(solution)/shard_map/ppermute | solution.py:15
  236.8 4.9 %copy-start.3 = (f32[768,160]{0,1:T(8,128)S(1)}, f32[768,160]{0,1:T(8,128)}, u32[]{:S(2)}) copy-start(f32[768,160]{0,1:T(8,128)} %get-tuple-element.52) | copy-start | bytes 1474564
  241.8 66.9 %copy-start.2 = (f32[768,160]{0,1:T(8,128)S(1)}, f32[768,160]{0,1:T(8,128)}, u32[]{:S(2)}) copy-start(f32[768,160]{0,1:T(8,128)} %param.20) | copy-start | bytes 1474564
  (23 other events, 56.2 us)
